TPU v7x, 256 devices: a whole 4x4x8 slice. The times are simulated.
256 devices in a mesh: arc: 4 (over x), row: 16 (over z, y_lo), col: 4 (over y_hi, core).
Axes of the slice: x: 4, y: 4 (y_hi: 2, y_lo: 2; y = y_hi * 2 + y_lo), z: 8, core: 2. Of those that a mesh axis runs over, the one named last changes fastest.
Arguments:
- local_normal: float32 [4, 512, 512], P('arc', None, 'col'), may hold values from -1 to 4, as said below
- link_block: float32 [4, 7424, 512], P('arc', 'row', 'col'), may hold values from -0.5 to 0.5
- local_rhs: float32 [4, 512], P('arc', 'col'), may hold values from -6 to 6
- arc_of_slot: int32 [4], P('arc'), may hold values from 0 to 3, each once
- live_params: int32 [4], replicated, may hold values from 256 to 512
Outputs:
- elimination_term: float32 [7424, 7424], P(('arc', 'col'), 'row')
- rhs_term: float32 [7424], P('row')
Inputs may be any that keep to these rules, and one draw needn't show every extreme that they name: `local_normal`: each slot's matrix is symmetric positive definite. `arc_of_slot`: each arc is held by exactly one slot.
All inputs are finite; a program needn't handle non-finite values.
Results may differ from a plain program's by a relative error of at most 0.0003.
Values sent between devices are 32-bit elements; how exact they have to be, the bound alone decides.
A program may use at most 64 MiB of HBM per device.

v0:
```python
import jax
import jax.numpy as jnp
from jax import lax
from jax.sharding import Mesh
from jax.sharding import PartitionSpec as P

ROW = ("row_0", "row_1")


def gathered_by_axis(x, axes, dim):
    result = x
    for number in range(len(axes) - 1, -1, -1):
        result = lax.all_gather(result, axes[number], axis=dim, tiled=True)
    return result


def shards(local_normal, link_block, local_rhs, arc_of_slot, live_params):
    order = local_normal.shape[1]
    width = local_normal.shape[2]
    column = lax.axis_index("col")
    arc_ids = jnp.arange(live_params.shape[0], dtype=jnp.int32)
    row_index = jnp.arange(order, dtype=jnp.int32)
    col_index = column * width + jnp.arange(width, dtype=jnp.int32)
    live = jnp.sum(jnp.where(arc_ids == arc_of_slot[0], live_params, 0))
    keep_rows = (row_index < live).astype(jnp.float32)
    keep_cols = (col_index < live).astype(jnp.float32)
    unit = (row_index[:, None] == col_index[None, :]).astype(jnp.float32)
    normal = (
        local_normal[0] * keep_rows[:, None] * keep_cols[None, :]
        + unit * (1.0 - keep_cols)[None, :]
    )
    link = link_block[0] * keep_cols[None, :]
    rhs = local_rhs[0] * keep_cols
    whole_normal = lax.all_gather(normal, "col", axis=1, tiled=True)
    whole_link = lax.all_gather(link, "col", axis=1, tiled=True)
    whole_rhs = lax.all_gather(rhs, "col", axis=0, tiled=True)
    factor = jnp.linalg.cholesky(whole_normal)
    reduced = jax.scipy.linalg.solve_triangular(factor, whole_link.T, lower=True).T
    solved = jax.scipy.linalg.solve_triangular(factor, whole_rhs, lower=True)
    own_panel = lax.dynamic_slice_in_dim(reduced, column * width, width, 1)
    own_solved = lax.dynamic_slice_in_dim(solved, column * width, width, 0)
    panel_list = [own_panel]
    solved_list = [own_solved]
    own_all = jnp.stack(panel_list)
    solved_all = jnp.stack(solved_list)
    rhs_local = jnp.einsum("srp,sp->r", own_all, solved_all, precision=lax.Precision.HIGHEST)
    gathered = gathered_by_axis(own_all, ROW, 1)
    elimination = lax.psum_scatter(
        jnp.einsum("sgp,srp->gr", gathered, own_all, precision=lax.Precision.HIGHEST),
        ("arc", "col"),
        scatter_dimension=0,
        tiled=True,
    )
    rhs_term = lax.psum(rhs_local, ("arc", "col"))
    return (elimination, rhs_term)


def solution(mesh):
    finer = Mesh(
        mesh.devices.reshape(mesh.shape["arc"], 8, 2, mesh.shape["col"]),
        ("arc", "row_0", "row_1", "col"),
    )
    in_specs = (P("arc", None, "col"), P("arc", ROW, "col"), P("arc", "col"), P("arc"), P())
    out_specs = (P(("arc", "col"), ROW), P(ROW))
    return jax.shard_map(
        shards, mesh=finer, in_specs=in_specs, out_specs=out_specs, check_vma=False
    )
```

profile of v0, /device:TPU:1, one launch (start us, length us, event | category | flops | bytes accessed | tf_op | source)
XLA Modules:
  0.0 404.6 jit_solution(15368856896345758970)
XLA Ops:
  7.9 1.4 fusion.52
  9.2 0.7 broadcast_subtract_fusion
  9.9 0.7 fusion.42
  10.6 1.1 copy.9
  11.7 0.8 fusion.17
  12.6 1.0 bitcast_multiply_fusion.1
  13.6 12.5 %all_gather.16 = f32[464,512]{1,0:T(8,128)S(1)} all-gather(f32[464,128]{1,0:T(8,128)S(1)} %bitcast_multiply_fusion.1), channel_id=1, replica_groups=mesh['arc'=4,'row_0'=8,'row_1'=2,'col'=4] {'col'}, dimensions={1}, use_global_device_ids=true | all-gather | bytes 1187840 | tf_op jit(solution)/shard_map/all_gather | solution.py:35
  26.1 14.1 %all-gather.6.cloned.1.call-done = f32[512,512]{0,1:T(8,128)} async-done(((f32[512,128]{0,1:T(8,128)}), f32[512,512]{0,1:T(8,128)}) %all-gather.6.cloned.1.call-update) | async-done | bytes 1048592 | tf_op jit(solution)/shard_map/all_gather | solution.py:34
  40.2 1.6 copy.10
  41.7 1.4 fusion.6
  43.2 1.0 copy-done
  44.2 11.7 %cholesky.104 = f32[128,128]{1,0:T(8,128)S(1)} custom-call(f32[128,128]{1,0:T(8,128)S(1)} %cholesky.266), custom_call_target="Cholesky" | custom-call | tf_op jit(solution)/shard_map/jit(cholesky)/cholesky | solution.py:37
  55.9 9.8 %custom-call.34 = f32[1,128,128]{1,2,0:T(8,128)S(1)} custom-call(f32[1,128,128]{2,1,0:T(8,128)S(1)} %get-tuple-element.31), custom_call_target="InvertDiagBlocksLowerTriangular" | custom-call | tf_op jit(solution)/shard_map/jit(cholesky)/cholesky | solution.py:37
  65.9 1.2 constant_dynamic-update-slice_fusion
  67.1 1.3 convolution_subtract_fusion.3
  68.4 11.7 %cholesky.217 = f32[128,128]{1,0:T(8,128)S(1)} custom-call(f32[128,128]{1,0:T(8,128)S(1)} %cholesky.270), custom_call_target="Cholesky" | custom-call | tf_op jit(solution)/shard_map/jit(cholesky)/cholesky | solution.py:37
  80.2 9.9 %custom-call.35 = f32[1,128,128]{1,2,0:T(8,128)S(1)} custom-call(f32[1,128,128]{2,1,0:T(8,128)S(1)} %get-tuple-element.28), custom_call_target="InvertDiagBlocksLowerTriangular" | custom-call | tf_op jit(solution)/shard_map/jit(cholesky)/cholesky | solution.py:37
  90.4 1.3 convolution_subtract_fusion.4
  91.7 11.7 %cholesky.238 = f32[128,128]{1,0:T(8,128)S(1)} custom-call(f32[128,128]{1,0:T(8,128)S(1)} %cholesky.275), custom_call_target="Cholesky" | custom-call | tf_op jit(solution)/shard_map/jit(cholesky)/cholesky | solution.py:37
  103.4 0.7 compare_reduce_fusion.1
  104.2 9.8 %custom-call.36 = f32[1,128,128]{1,2,0:T(8,128)S(1)} custom-call(f32[1,128,128]{2,1,0:T(8,128)S(1)} %get-tuple-element.25), custom_call_target="InvertDiagBlocksLowerTriangular" | custom-call | tf_op jit(solution)/shard_map/jit(cholesky)/cholesky | solution.py:37
  114.2 1.2 convolution_subtract_fusion.5
  115.4 11.8 %cholesky.255 = f32[128,128]{1,0:T(8,128)S(1)} custom-call(f32[128,128]{1,0:T(8,128)S(1)} %convolution_subtract_fusion.5), custom_call_target="Cholesky" | custom-call | tf_op jit(solution)/shard_map/jit(cholesky)/cholesky | solution.py:37
  127.3 0.7 compare_reduce_fusion
  128.0 0.6 compare_reduce_fusion.2
  131.4 8.5 %while.1 = (s32[]{:T(128)}, f32[512,512]{1,0:T(8,128)S(1)}, s32[4,2]{0,1:T(2,128)S(1)}, f32[4,128,128]{2,1,0:T(8,128)S(1)}, s32[]{:T(128)}) while((s32[]{:T(128)}, f32[512,512]{1,0:T(8,128)S(1)}, s32[4,2]{0,1:T(2,128)S(1)}, f32[4,128,128]{2,1,0:T(8,128)S(1)}, s32[]{:T(128)}) %tuple.32), condition=%wide.while_cond, body=%wide.while_body.sunk | while | flops 2 | bytes 131189 | solution.py:38
  131.5 0.6 fusion.80
  132.1 1.4 bitcast_dynamic-update-slice_fusion.2
  133.6 0.6 fusion.80
  134.2 1.4 bitcast_dynamic-update-slice_fusion.2
  135.7 0.6 fusion.80
  136.3 1.4 bitcast_dynamic-update-slice_fusion.2
  137.8 0.6 fusion.80
  138.4 1.4 bitcast_dynamic-update-slice_fusion.2
  139.9 39.3 %custom-call.37 = f32[4,128,128]{1,2,0:T(8,128)S(1)} custom-call(f32[4,128,128]{2,1,0:T(8,128)S(1)} %get-tuple-element.9), custom_call_target="InvertDiagBlocksLowerTriangular" | custom-call | tf_op jit(solution)/shard_map/jit(_solve_triangular)/triangular_solve | solution.py:38
  179.2 0.3 fusion.21
  179.5 0.4 convolution_subtract_fusion.2
  180.3 0.5 convolution_subtract_fusion.1
  181.2 0.8 convolution_subtract_fusion
  182.4 7.8 %all-gather = f32[928,128]{1,0:T(8,128)} all-gather(f32[464,128]{1,0:T(8,128)S(1)} %bitcast.137), channel_id=2, replica_groups=mesh['arc'=4,'row_0'=8,'row_1'=2,'col'=4] {'row_1'}, dimensions={0}, use_global_device_ids=true | all-gather | bytes 712704 | tf_op jit(solution)/shard_map/all_gather | solution.py:13
  190.3 50.9 %all-gather.8.cloned.1.call-done = f32[7424,128]{1,0:T(8,128)} async-done(((f32[928,128]{1,0:T(8,128)}), f32[7424,128]{1,0:T(8,128)}) %all-gather.8.cloned.1.call-update) | async-done | bytes 3801104 | tf_op jit(solution)/shard_map/all_gather | solution.py:13
  241.2 15.9 %fusion.67 = f32[7424,464]{1,0:T(8,128)} fusion(f32[7424,128]{1,0:T(8,128)} %all-gather.8.cloned.1.call-done, f32[128,464]{0,1:T(8,128)S(1)} %fusion.20), kind=kOutput, calls=%fused_computation.127 | convolution fusion | flops 5291114496 | bytes 17817600 | tf_op jit(solution)/shard_map/sgp,srp->gr/dot_general | solution.py:49
  257.2 0.6 copy-done.1
  257.8 0.7 fusion.51
  258.5 7.2 %all-gather.2 = f32[4,1,128]{2,1,0:T(1,128)S(1)} all-gather(f32[1,1,128]{2,1,0:T(1,128)S(1)} %fusion.51), channel_id=1, replica_groups=mesh['arc'=4,'row_0'=8,'row_1'=2,'col'=4] {'col'}, dimensions={0}, use_global_device_ids=true | all-gather | bytes 2560 | tf_op jit(solution)/shard_map/all_gather | solution.py:36
  267.2 0.4 fusion.55
  267.6 33.3 %psum.7 = f32[464]{0:T(512)} all-reduce(f32[464]{0:T(512)S(1)} %bitcast.138), channel_id=1, replica_groups=mesh['arc'=4,'row_0'=8,'row_1'=2,'col'=4] {'arc','col'}, use_global_device_ids=true, to_apply=%region_10.11 | all-reduce | flops 464 | bytes 3712 | tf_op jit(solution)/shard_map/psum | solution.py:54
  300.8 97.2 %reduce-scatter.2.cloned.1.call-done = f32[464,464]{1,0:T(8,128)} async-done(((f32[7424,464]{1,0:T(8,128)}), f32[464,464]{1,0:T(8,128)}) %reduce-scatter.2.cloned.1.call-update) | async-done | bytes 861200 | tf_op jit(solution)/shard_map/reduce_scatter | solution.py:48
  (38 shorter events, 3.9 us)
Async XLA Ops:
  7.2 33.0 %all-gather.6.cloned.1.call-start = ((), (), s32[]{:S(2)}) async-start(), calls=%async_computation.1 | async-start | bytes 1310720 | tf_op jit(solution)/shard_map/all_gather | solution.py:34
  12.5 228.7 %all-gather.8.cloned.1.call-start = ((), (), s32[]{:S(2)}) async-start(), calls=%async_computation.3 | async-start | bytes 4276224 | tf_op jit(solution)/shard_map/all_gather | solution.py:13
  43.2 1.0 copy-start
  190.3 207.8 %reduce-scatter.2.cloned.1.call-start = ((), (), s32[]{:S(2)}) async-start(), calls=%async_computation.2 | async-start | bytes 16154624 | tf_op jit(solution)/shard_map/reduce_scatter | solution.py:48
  257.2 0.7 copy-start.1
Sparse Core Ops, SparseCore 0:
  12.7 27.4 all-gather.5
  190.4 50.7 all-gather.7
  257.3 140.6 reduce-scatter.1
where the time goes:
time: 405 us
  waiting for transfers between devices  162 us (40%)
  other arithmetic  125 us (31%)
  blocking collectives  60.9 us (15%)
  matrix products  26.3 us (6%)
  between operations  17.3 us (4%)
  local copies, waits for them, and re-layouts  12.8 us (3%)
    reduce_scatter x1, waiting for transfers between devices, shards(): lax.psum_scatter(jnp.einsum('sgp,srp->gr', gathered, own_all, precision=l...  97.2 us
    another operation x14, other arithmetic, shards(): factor = jnp.linalg.cholesky(whole_normal)  78.8 us
    all_gather x1, waiting for transfers between devices, gathered_by_axis(): result = lax.all_gather(result, axes[number], axis=dim, tiled=True)  50.9 us
    another operation x4, other arithmetic, shards(): jax.scipy.linalg.solve_triangular(factor, whole_link.T, lower=True)  39.5 us
    psum x1, blocking collectives, shards(): rhs_term = lax.psum(rhs_local, ('arc', 'col'))  33.3 us
    dot_general x1, matrix products, shards(): jnp.einsum('sgp,srp->gr', gathered, own_all, precision=lax.Precision.HIGH...  15.9 us
    all_gather x1, waiting for transfers between devices, shards(): whole_normal = lax.all_gather(normal, 'col', axis=1, tiled=True)  14.1 us
    all_gather x1, blocking collectives, shards(): whole_link = lax.all_gather(link, 'col', axis=1, tiled=True)  12.5 us
  transfers between devices with their start and end apart: 3, of which 3 were waited for; matrix products, arithmetic and copies ran while one was open for 1% of the time, Pallas kernels for 0%

commit v1 on v0

v1 whole, which is shorter than its diff:
```python
import functools

import jax
import jax.numpy as jnp
from jax import lax
from jax.experimental import pallas as pl
from jax.experimental.pallas import tpu as pltpu
from jax.sharding import PartitionSpec as P

HI = lax.Precision.HIGHEST
F32 = jnp.float32
BF16 = jnp.bfloat16
UNITS = 2


def small_inverse(cols):
    s = lax.broadcasted_iota(jnp.int32, (1, 8, 128), 1)
    j = lax.broadcasted_iota(jnp.int32, (8, 1, 1), 0)
    for k in range(8):
        p = 1.0 / cols[k : k + 1, k : k + 1, :]
        f = jnp.where(j == k, p, cols[:, k : k + 1, :] * p)
        ck = jnp.where(s == k, -1.0, cols[k : k + 1])
        cols = jnp.where((s == k) | (j == k), 0.0, cols) - ck * f
    return cols


def block_inverse(a, tick):
    n = 128
    lane = lax.broadcasted_iota(jnp.int32, (1, n), 1)
    for g in range(n // 8):
        k = 8 * g
        rows = a[k : k + 8, :]
        cols = jnp.stack(
            [jnp.broadcast_to(rows[:, k + j : k + j + 1], (8, n)) for j in range(8)]
        )
        inv = small_inverse(cols)
        q = inv[0] * rows[0:1, :]
        for j in range(1, 8):
            q = q + inv[j] * rows[j : j + 1, :]
        for j in range(8):
            q = jnp.where(lane == k + j, inv[j], q)
        rest = jnp.where((lane >= k) & (lane < k + 8), 0.0, a)
        for j in range(8):
            rest = rest - a[:, k + j : k + j + 1] * q[j : j + 1, :]
        parts = [q]
        if k:
            parts.insert(0, rest[:k])
        if k + 8 < n:
            parts.append(rest[k + 8 :])
        a = jnp.concatenate(parts, 0)
        tick()
    return a


def invert(work, tick):
    for g in range(4):
        ks = slice(128 * g, 128 * g + 128)
        p = block_inverse(work[g, ks, :], tick)
        rows = [
            p
            if c == g
            else jnp.dot(p, work[c, ks, :], precision=HI, preferred_element_type=F32)
            for c in range(4)
        ]
        for t in range(4):
            if t == g:
                continue
            ts = slice(128 * t, 128 * t + 128)
            a = work[g, ts, :]
            for c in range(4):
                d = jnp.dot(a, rows[c], precision=HI, preferred_element_type=F32)
                work[c, ts, :] = -d if c == g else work[c, ts, :] - d
        for c in range(4):
            work[c, ks, :] = rows[c]


def split(v):
    high = v.astype(BF16)
    return high, (v - high.astype(F32)).astype(BF16)


def dot3(a, b, dims):
    ah, al = a
    bh, bl = b
    dn = (dims, ((), ()))
    return (
        lax.dot_general(ah, bh, dn, preferred_element_type=F32)
        + lax.dot_general(ah, bl, dn, preferred_element_type=F32)
        + lax.dot_general(al, bh, dn, preferred_element_type=F32)
    )


def kernel(
    arc_ref, live_ref, n_ref, l_ref, r_ref, out_ref, rhs_ref,
    panels, rpanels, work, ja, jb, ia, ib, inv, ah, al, bh, bl, nh, nl, wh, wl, tile, other,
    n_send, n_recv, r_send, r_recv, j_send, j_recv, jp_send, jp_recv,
    z_send, z_recv, ip_send, ip_recv, v_send, v_recv, vp_send, vp_recv, t_send, t_recv, local,
):
    x = lax.axis_index("arc")
    row = lax.axis_index("row")
    col = lax.axis_index("col")
    z, l = lax.div(row, 2), lax.rem(row, 2)
    h, b = lax.div(col, 2), lax.rem(col, 2)
    y = 2 * h + l
    home = 2 * x + h
    rows = l_ref.shape[0]
    part = rows // UNITS

    def device(dx=0, dy=0, dz=0, db=0):
        yy = lax.rem(y + dy + 4, 4)
        zz = lax.rem(z + dz + 8, 8)
        bb = lax.rem(b + db, 2)
        return {
            "arc": lax.rem(x + dx + 4, 4),
            "row": 2 * zz + lax.rem(yy, 2),
            "col": 2 * lax.div(yy, 2) + bb,
        }

    def remote(src, dst, ss, rs, dev):
        return pltpu.make_async_remote_copy(
            src_ref=src, dst_ref=dst, send_sem=ss, recv_sem=rs,
            device_id=dev, device_id_type=pl.DeviceIdType.MESH,
        )

    here = {"arc": x, "row": row, "col": col}
    swap_to = {"arc": x, "row": 2 * z + (1 - l), "col": 2 * h + (1 - b)}
    partner = device(db=1)

    barrier = pltpu.get_barrier_semaphore()
    peers = [device(dx=d) for d in (1, 2, 3)] + [device(dy=d) for d in (1, 2, 3)]
    peers += [device(dz=1), device(dz=7), partner, swap_to]
    for p in peers:
        pl.semaphore_signal(barrier, inc=1, device_id=p, device_id_type=pl.DeviceIdType.MESH)
    pl.semaphore_wait(barrier, len(peers))

    own_c = col
    far_c = 2 * (1 - h) + b
    mate_c = 2 * h + (1 - b)
    last_c = 2 * (1 - h) + (1 - b)

    def n_copy(i, slot, dev):
        return remote(panels.at[slot], panels.at[slot], n_send.at[i], n_recv.at[i], dev)

    def r_copy(i, slot, dev):
        return remote(rpanels.at[slot], rpanels.at[slot], r_send.at[i], r_recv.at[i], dev)

    def along(e, d):
        return e * (1 - b) + d * b, e * b + d * (1 - b)

    def slot_of(dx, dy):
        return lax.rem(x - dx + 8, 4), lax.rem(y - dy + 8, 4)

    def j_first(e):
        dx, dy = along(e, 0)
        return remote(l_ref, ja.at[x, y], j_send.at[e], j_recv.at[e * 4], device(dx, dy))

    def j_second(e, d):
        sx, sy = slot_of(*along(e, 0))
        dx, dy = along(0, d)
        src = l_ref if e == 0 else ja.at[sx, sy]
        return remote(src, ja.at[sx, sy], j_send.at[4 + e * 4 + d], j_recv.at[e * 4 + d], device(dx, dy))

    def j_wait(e, d):
        dx, dy = along(e, d)
        sx, sy = slot_of(dx, dy)
        remote(l_ref, ja.at[sx, sy], j_send.at[0], j_recv.at[e * 4 + d], here).wait_recv()

    def jp_copy(sx, sy):
        return remote(
            ja.at[sx, sy], jb.at[sx, lax.div(sy, 2)],
            jp_send.at[sx, lax.div(sy, 2)], jp_recv.at[sx, lax.div(sy, 2)], partner,
        )

    def j_pass(e, d):
        sx, sy = slot_of(*along(e, d))

        @pl.when(lax.rem(sy, 2) != b)
        def _():
            jp_copy(sx, sy).start()

    t_up = lax.rem(z - home + 8, 8)
    t_down = lax.rem(home - z + 8, 8)
    n_units = 4 * UNITS

    def z_slot(up, n):
        p, u = lax.div(n, UNITS), lax.rem(n, UNITS)
        dx = lax.rem(p, 2) if up else 3 - lax.rem(p, 2)
        dy = 2 * lax.div(p, 2)
        sx, sy = slot_of(dx, dy)
        return sx, lax.div(sy, 2), sy, pl.ds(u * part, part)

    def z_copy(up, n, source):
        sx, sh, sy, cut = z_slot(up, n)
        src = ja.at[sx, sy, cut] if source else ia.at[sx, sh, cut]
        k = 0 if up else 1
        return remote(
            src, ia.at[sx, sh, cut], z_send.at[k, n], z_recv.at[k, n], device(dz=1 if up else 7)
        )

    def z_step(up, m):
        t = t_up if up else t_down
        n = m - t

        @pl.when((n >= 0) & (n < n_units))
        def _():
            @pl.when(t == 0)
            def _():
                z_copy(up, n, True).start()

            @pl.when(t > 0)
            def _():
                z_copy(up, n, False).wait_recv()

                @pl.when(t < 7)
                def _():
                    z_copy(up, n, False).start()

    def i_local(sx, sh):
        return pltpu.make_async_copy(ja.at[sx, 2 * sh + l], ia.at[sx, sh], local.at[sx, sh])

    def ip_copy(sx, sh):
        return remote(ia.at[sx, sh], ib.at[sx, sh], ip_send.at[sx, sh], ip_recv.at[sx, sh], partner)

    own_local = pltpu.make_async_copy(l_ref, ja.at[x, y], local.at[4, 0])
    own_local.start()
    panels[own_c] = n_ref[...]
    rpanels[own_c] = r_ref[...]
    to_far = remote(n_ref, panels.at[own_c], n_send.at[0], n_recv.at[0], device(dy=2))
    to_mate = remote(n_ref, panels.at[own_c], n_send.at[1], n_recv.at[1], partner)
    rto_far = remote(r_ref, rpanels.at[own_c], r_send.at[0], r_recv.at[0], device(dy=2))
    rto_mate = remote(r_ref, rpanels.at[own_c], r_send.at[1], r_recv.at[1], partner)
    for c in (to_far, rto_far, to_mate, rto_mate):
        c.start()
    for e in (1, 3, 2):
        j_first(e).start()
    for d in (1, 3, 2):
        j_second(0, d).start()

    n_copy(0, far_c, here).wait_recv()
    r_copy(0, far_c, here).wait_recv()
    n_copy(2, far_c, partner).start()
    r_copy(2, far_c, partner).start()
    own_local.wait()
    n_copy(1, mate_c, here).wait_recv()
    r_copy(1, mate_c, here).wait_recv()
    n_copy(2, last_c, here).wait_recv()
    r_copy(2, last_c, here).wait_recv()

    live = live_ref[arc_ref[0]]
    sub = lax.broadcasted_iota(jnp.int32, (512, 128), 0)
    lane = lax.broadcasted_iota(jnp.int32, (512, 128), 1)
    for c in range(4):
        ident = jnp.where(sub == lane + 128 * c, 1.0, 0.0)
        keep = (sub < live) & (lane + 128 * c < live)
        work[c] = jnp.where(keep, panels[c], ident)

    events = []
    for e in (1, 3, 2):
        def first_arrival(e=e):
            j_wait(e, 0)
            for d in (1, 3, 2):
                j_second(e, d).start()
        events.append(first_arrival)

    waited = {(0, 0), (1, 0), (2, 0), (3, 0)}
    for m in range(n_units + 7):
        if m % UNITS == 0 and m // UNITS < 4:
            p = m // UNITS
            for dx in (p % 2, 3 - p % 2):
                dy = 2 * (p // 2)
                def arrive(dx=dx, dy=dy):
                    if (dx, dy) not in waited:
                        @pl.when(b == 0)
                        def _():
                            remote(l_ref, ja.at[0, 0], j_send.at[0], j_recv.at[dx * 4 + dy], here).wait_recv()
                    if (dy, dx) not in waited:
                        @pl.when(b == 1)
                        def _():
                            remote(l_ref, ja.at[0, 0], j_send.at[0], j_recv.at[dy * 4 + dx], here).wait_recv()

                events.append(arrive)

        def ring(m=m):
            z_step(True, m)
            z_step(False, m)

        events.append(ring)

    state = {"ticks": 0, "done": 0}

    def tick():
        state["ticks"] += 1
        if state["ticks"] % 2 == 0 and state["done"] < len(events):
            events[state["done"]]()
            state["done"] += 1

    invert(work, tick)
    while state["done"] < len(events):
        events[state["done"]]()
        state["done"] += 1

    v = [jnp.zeros((8, 128), F32) for _ in range(4)]
    for c in range(4):
        keep = (sub < live) & (lane + 128 * c < live)
        w = jnp.where(keep, work[c], 0.0)
        inv[x, c, 0:512, :] = w
        for t in range(4):
            r8 = jnp.broadcast_to(rpanels[t], (8, 128))
            v[c] = v[c] + jnp.dot(
                r8, w[128 * t : 128 * t + 128, :], precision=HI, preferred_element_type=F32
            )
    for c in range(4):
        inv[x, c, 512:520, :] = v[c]

    half = pl.ds(2 * b, 2)
    rest = pl.ds(2 * (1 - b), 2)

    def v_copy(d):
        return remote(inv.at[x, half], inv.at[x, half], v_send.at[d], v_recv.at[d], device(dx=d))

    def v_arrive(d):
        s = lax.rem(x - d + 4, 4)
        return remote(inv.at[s, half], inv.at[s, half], v_send.at[0], v_recv.at[d], here)

    def v_pass(d):
        s = lax.rem(x - d + 4, 4)
        return remote(inv.at[s, half], inv.at[s, half], vp_send.at[d], vp_recv.at[d], partner)

    def v_passed(d):
        s = lax.rem(x - d + 4, 4)
        return remote(inv.at[s, rest], inv.at[s, rest], vp_send.at[0], vp_recv.at[d], here)

    for d in (1, 3, 2):
        v_copy(d).start()

    order0 = {(p % 2, 2 * (p // 2)) for p in range(4)} | {(3 - p % 2, 2 * (p // 2)) for p in range(4)}
    for e in range(4):
        for d in range(4):
            if (e, d) in waited:
                continue

            @pl.when((b == 0) & ((e, d) not in order0) | (b == 1) & ((d, e) not in order0))
            def _():
                j_wait(e, d)

    for sx in range(4):
        for sh in range(2):
            @pl.when(z == home)
            def _():
                i_local(sx, sh).start()

            jp_copy(sx, 2 * sh + (1 - b)).start()
    for sx in range(4):
        for sh in range(2):
            @pl.when(z == home)
            def _():
                i_local(sx, sh).wait()

            ip_copy(sx, sh).start()
    for sx in range(4):
        for sh in range(2):
            remote(ja.at[sx, 0], jb.at[sx, sh], jp_send.at[0, 0], jp_recv.at[sx, sh], here).wait_recv()
            remote(ja.at[sx, 0], ib.at[sx, sh], ip_send.at[0, 0], ip_recv.at[sx, sh], here).wait_recv()

    tile[...] = jnp.zeros_like(tile)
    chunk = [2 * 0 + b, 2 * 1 + b, 2 * 0 + (1 - b), 2 * 1 + (1 - b)]

    for d in (0, 1, 3, 2):
        s = lax.rem(x - d + 4, 4)
        if d:
            v_arrive(d).wait_recv()
            v_pass(d).start()
            v_passed(d).wait_recv()
        for p in range(4):
            at = slice(128 * p, 128 * p + 128)
            src_i = ia if p < 2 else ib
            high, low = split(src_i[s, p % 2])
            ah[:, at], al[:, at] = high, low
            src_j = ja[s, 2 * p + b] if p < 2 else jb[s, p - 2]
            high, low = split(src_j)
            bh[:, at], bl[:, at] = high, low
            for q in range(4):
                to = slice(128 * q, 128 * q + 128)
                high, low = split(inv[s, chunk[q], pl.ds(128 * chunk[p], 128), :])
                nh[at, to], nl[at, to] = high, low
        w = dot3((ah[...], al[...]), (nh[...], nl[...]), ((1,), (0,)))
        high, low = split(w)
        wh[0:rows], wl[0:rows] = high, low
        for q in range(4):
            to = slice(128 * q, 128 * q + 128)
            high, low = split(jnp.broadcast_to(inv[s, chunk[q], 512:513, :], (16, 128)))
            wh[rows : rows + 16, to], wl[rows : rows + 16, to] = high, low
        tile[...] += dot3((wh[...], wl[...]), (bh[...], bl[...]), ((1,), (1,)))

    swap = remote(tile, other, t_send.at[0], t_recv.at[0], swap_to)
    big = lambda src: pltpu.make_async_copy(src.at[0:rows], out_ref, local.at[4, 0])
    little = lambda src: pltpu.make_async_copy(src.at[rows : rows + 8], rhs_ref, local.at[4, 1])

    @pl.when(l != b)
    def _():
        swap.start()
        swap.wait()
        big(other).start()
        little(other).start()
        big(other).wait()
        little(other).wait()

    @pl.when(l == b)
    def _():
        big(tile).start()
        little(tile).start()
        big(tile).wait()
        little(tile).wait()

    to_far.wait_send()
    to_mate.wait_send()
    rto_far.wait_send()
    rto_mate.wait_send()
    n_copy(2, far_c, partner).wait_send()
    r_copy(2, far_c, partner).wait_send()
    for e in (1, 2, 3):
        j_first(e).wait_send()
    for e in range(4):
        for d in (1, 2, 3):
            j_second(e, d).wait_send()
    for sx in range(4):
        for sh in range(2):
            jp_copy(sx, 2 * sh + (1 - b)).wait_send()
            ip_copy(sx, sh).wait_send()
    for n in range(n_units):
        for up in (True, False):
            @pl.when((t_up if up else t_down) < 7)
            def _():
                z_copy(up, n, False).wait_send()
    for d in (1, 2, 3):
        v_copy(d).wait_send()
        v_pass(d).wait_send()


def shards(local_normal, link_block, local_rhs, arc_of_slot, live_params):
    order, width = local_normal.shape[1:]
    rows = link_block.shape[1]
    vmem = pl.BlockSpec(memory_space=pltpu.VMEM)
    smem = pl.BlockSpec(memory_space=pltpu.SMEM)
    dma = pltpu.SemaphoreType.DMA
    piece = (rows, width)
    half = (4, 2) + piece
    tile, vector = pl.pallas_call(
        kernel,
        out_shape=(
            jax.ShapeDtypeStruct((rows, rows), F32),
            jax.ShapeDtypeStruct((8, rows), F32),
        ),
        in_specs=[smem, smem, vmem, vmem, vmem],
        out_specs=(pl.BlockSpec(memory_space=pl.ANY),) * 2,
        scratch_shapes=[
            pltpu.VMEM((4, order, width), F32),
            pltpu.VMEM((4, 1, width), F32),
            pltpu.VMEM((4, order, width), F32),
            pltpu.VMEM((4, 4) + piece, F32),
            pltpu.VMEM(half, F32),
            pltpu.VMEM(half, F32),
            pltpu.VMEM(half, F32),
            pltpu.VMEM((4, 4, order + 8, width), F32),
            pltpu.VMEM((rows, order), BF16),
            pltpu.VMEM((rows, order), BF16),
            pltpu.VMEM((rows, order), BF16),
            pltpu.VMEM((rows, order), BF16),
            pltpu.VMEM((order, order), BF16),
            pltpu.VMEM((order, order), BF16),
            pltpu.VMEM((rows + 16, order), BF16),
            pltpu.VMEM((rows + 16, order), BF16),
            pltpu.VMEM((rows + 16, rows), F32),
            pltpu.VMEM((rows + 16, rows), F32),
            dma((3,)), dma((3,)), dma((3,)), dma((3,)),
            dma((20,)), dma((16,)), dma((4, 2)), dma((4, 2)),
            dma((2, 4 * UNITS)), dma((2, 4 * UNITS)), dma((4, 2)), dma((4, 2)),
            dma((4,)), dma((4,)), dma((4,)), dma((4,)), dma((1,)), dma((1,)), dma((5, 2)),
        ],
        compiler_params=pltpu.CompilerParams(
            collective_id=0, has_side_effects=True, vmem_limit_bytes=56 * 2**20
        ),
        name="eliminate",
    )(arc_of_slot, live_params, local_normal[0], link_block[0], local_rhs)
    return tile, vector[0]


def solution(mesh):
    in_specs = (P("arc", None, "col"), P("arc", "row", "col"), P("arc", "col"), P("arc"), P())
    out_specs = (P(("arc", "col"), "row"), P("row"))
    return jax.shard_map(
        shards, mesh=mesh, in_specs=in_specs, out_specs=out_specs, check_vma=False
    )
```

time: 405 us -> 143 us (0.35)
  the two profiles are of different devices: /device:TPU:1 before, /device:TPU:24 now
where the time goes in v1:
time: 143 us; the launch traced here: 142 us
  Pallas kernels  138 us (97%)
  local copies, waits for them, and re-layouts  3.48 us (2%)
    pallas_call x1, Pallas kernels, shards(): pl.pallas_call(kernel, out_shape=(jax.ShapeDtypeStruct((rows, rows), F32)...  138 us

profile of v1, /device:TPU:24, one launch (start us, length us, event | category | flops | bytes accessed | tf_op | source)
XLA Modules:
  0.0 142.4 jit_solution(7947326536595953826)
XLA Ops:
  1.3 137.7 %eliminate.1 = (f32[464,464]{1,0:T(8,128)}, f32[8,464]{1,0:T(8,128)}) custom-call(s32[1]{0:T(128)S(6)} %copy.8.arc_ref, s32[4]{0:T(128)} %live_ref.1, f32[512,128]{1,0:T(8,128)} %bitcast.3, f32[464,128]{1,0:T(8,128)} %bitcast.4, f32[1,128]{1,0:T(1,128)} %r_ref.1), custom_call_target="tpu_custom_call" | custom-call | tf_op jit(solution)/shard_map/eliminate/pallas_call | solution.py:448
  139.0 1.3 slice.3
  140.3 2.2 %copy.9 = f32[464,464]{1,0:T(8,128)} copy(f32[464,464]{1,0:T(8,128)} %get-tuple-element.8) | data formatting | bytes 1722368

commit v2 on v1

v2 whole, which is shorter than its diff:
```python
import functools

import jax
import jax.numpy as jnp
from jax import lax
from jax.experimental import pallas as pl
from jax.experimental.pallas import tpu as pltpu
from jax.sharding import PartitionSpec as P

HI = lax.Precision.HIGHEST
F32 = jnp.float32
BF16 = jnp.bfloat16
UNITS = 8
LAG = 4
PACK = (((0, 0), (1, 0), (2, 0), (3, 0), (3, 3)), ((1, 1), (2, 1), (3, 1), (2, 2), (3, 2)))


def small_inverse(cols):
    s = lax.broadcasted_iota(jnp.int32, (1, 8, 128), 1)
    j = lax.broadcasted_iota(jnp.int32, (8, 1, 1), 0)
    for k in range(8):
        p = 1.0 / cols[k : k + 1, k : k + 1, :]
        f = jnp.where(j == k, p, cols[:, k : k + 1, :] * p)
        ck = jnp.where(s == k, -1.0, cols[k : k + 1])
        cols = jnp.where((s == k) | (j == k), 0.0, cols) - ck * f
    return cols


def block_inverse(a, tick):
    n = 128
    lane = lax.broadcasted_iota(jnp.int32, (1, n), 1)
    for g in range(n // 8):
        k = 8 * g
        rows = a[k : k + 8, :]
        cols = jnp.stack(
            [jnp.broadcast_to(rows[:, k + j : k + j + 1], (8, n)) for j in range(8)]
        )
        inv = small_inverse(cols)
        q = inv[0] * rows[0:1, :]
        for j in range(1, 8):
            q = q + inv[j] * rows[j : j + 1, :]
        for j in range(8):
            q = jnp.where(lane == k + j, inv[j], q)
        rest = jnp.where((lane >= k) & (lane < k + 8), 0.0, a)
        for j in range(8):
            rest = rest - a[:, k + j : k + j + 1] * q[j : j + 1, :]
        parts = [q]
        if k:
            parts.insert(0, rest[:k])
        if k + 8 < n:
            parts.append(rest[k + 8 :])
        a = jnp.concatenate(parts, 0)
        tick()
    return a


def invert(work, tick):
    for g in range(4):
        ks = slice(128 * g, 128 * g + 128)
        p = block_inverse(work[g, ks, :], tick)
        rows = [
            p
            if c == g
            else jnp.dot(p, work[c, ks, :], precision=HI, preferred_element_type=F32)
            for c in range(4)
        ]
        for t in range(4):
            if t == g:
                continue
            ts = slice(128 * t, 128 * t + 128)
            a = work[g, ts, :]
            for c in range(4):
                d = jnp.dot(a, rows[c], precision=HI, preferred_element_type=F32)
                work[c, ts, :] = -d if c == g else work[c, ts, :] - d
        for c in range(4):
            work[c, ks, :] = rows[c]


def split(v):
    high = v.astype(BF16)
    return high, (v - high.astype(F32)).astype(BF16)


def dot3(a, b, dims):
    ah, al = a
    bh, bl = b
    dn = (dims, ((), ()))
    return (
        lax.dot_general(ah, bh, dn, preferred_element_type=F32)
        + lax.dot_general(ah, bl, dn, preferred_element_type=F32)
        + lax.dot_general(al, bh, dn, preferred_element_type=F32)
    )


def kernel(
    arc_ref, live_ref, n_ref, l_ref, r_ref, out_ref, rhs_ref,
    panels, rp, work, jj, ii, pk, ah, al, bh, bl, nh, nl, wh, wl, tile, other,
    n_send, n_recv, r_send, r_recv, rx_send, rx_recv, d_send, d_recv, j_send, j_recv,
    jp_send, jp_recv, z_send, z_recv, ip_send, ip_recv,
    v_send, v_recv, vp_send, vp_recv, t_send, t_recv, local,
):
    x = lax.axis_index("arc")
    row = lax.axis_index("row")
    col = lax.axis_index("col")
    z, l = lax.div(row, 2), lax.rem(row, 2)
    h, b = lax.div(col, 2), lax.rem(col, 2)
    y = 2 * h + l
    home = 2 * x + h
    at_home = z == home
    rows = l_ref.shape[0]

    def device(dx=0, dy=0, dz=0, db=0):
        yy = lax.rem(y + dy + 4, 4)
        zz = lax.rem(z + dz + 8, 8)
        bb = lax.rem(b + db, 2)
        return {
            "arc": lax.rem(x + dx + 4, 4),
            "row": 2 * zz + lax.rem(yy, 2),
            "col": 2 * lax.div(yy, 2) + bb,
        }

    def remote(src, dst, ss, rs, dev):
        return pltpu.make_async_remote_copy(
            src_ref=src, dst_ref=dst, send_sem=ss, recv_sem=rs,
            device_id=dev, device_id_type=pl.DeviceIdType.MESH,
        )

    here = {"arc": x, "row": row, "col": col}
    swap_to = {"arc": x, "row": 2 * z + (1 - l), "col": 2 * h + (1 - b)}
    source = {"arc": lax.div(z, 2), "row": row, "col": 2 * lax.rem(z, 2) + b}
    partner = device(db=1)

    barrier = pltpu.get_barrier_semaphore()
    peers = [device(dx=d) for d in (1, 2, 3)] + [device(dy=d) for d in (1, 2, 3)]
    peers += [device(dx=d, dy=2) for d in (1, 2, 3)]
    peers += [device(dz=1), device(dz=7), partner, swap_to]
    for p in peers:
        pl.semaphore_signal(barrier, inc=1, device_id=p, device_id_type=pl.DeviceIdType.MESH)
    pl.semaphore_wait(barrier, len(peers))

    far_c = 2 * (1 - h) + b
    mate_c = 2 * h + (1 - b)
    last_c = 2 * (1 - h) + (1 - b)

    def n_own(i, dev):
        return remote(n_ref, panels.at[col], n_send.at[i], n_recv.at[i], dev)

    def n_copy(i, slot, dev):
        return remote(panels.at[slot], panels.at[slot], n_send.at[i], n_recv.at[i], dev)

    def r_own(i, dev):
        return remote(r_ref, rp.at[x, col], r_send.at[i], r_recv.at[i], dev)

    def r_copy(i, slot, dev):
        return remote(rp.at[x, slot], rp.at[x, slot], r_send.at[i], r_recv.at[i], dev)

    def rx_copy(d):
        return remote(rp.at[x], rp.at[x], rx_send.at[d], rx_recv.at[d], device(dx=d))

    def along(e, d):
        return e * (1 - b) + d * b, e * b + d * (1 - b)

    def slot_of(dx, dy):
        return lax.rem(x - dx + 8, 4), lax.rem(y - dy + 8, 4)

    def j_at(sx, sy):
        return jj.at[sx, 2 * lax.div(sy, 2) + b, lax.rem(sy, 2)]

    def j_first(e):
        dx, dy = along(e, 0)
        return remote(l_ref, j_at(x, y), j_send.at[e], j_recv.at[e * 4], device(dx, dy))

    def j_second(e, d):
        sx, sy = slot_of(*along(e, 0))
        dx, dy = along(0, d)
        src = l_ref if e == 0 else j_at(sx, sy)
        return remote(src, j_at(sx, sy), j_send.at[4 + e * 4 + d], j_recv.at[e * 4 + d], device(dx, dy))

    def jp_copy(sx, sh):
        at = jj.at[sx, 2 * sh + b, 1 - b]
        return remote(at, at, jp_send.at[sx, sh], jp_recv.at[sx, sh], partner)

    def j_arrive(e, d):
        dx, dy = along(e, d)
        sx, sy = slot_of(dx, dy)
        if e or d:
            remote(l_ref, j_at(sx, sy), j_send.at[0], j_recv.at[e * 4 + d], here).wait_recv()

        @pl.when(lax.rem(sy, 2) != b)
        def _():
            jp_copy(sx, lax.div(sy, 2)).start()

    t_up = lax.rem(z - home + 8, 8)
    t_down = lax.rem(home - z + 8, 8)
    n_units = 4 * UNITS
    quarter = rows // 2 // 4 // 8 * 8
    sizes = (rows // 2 - 3 * quarter, quarter, quarter, quarter)

    def z_piece(up, p):
        dx = lax.rem(p, 2) if up else 3 - lax.rem(p, 2)
        sx, sy = slot_of(dx, 2 * lax.div(p, 2))
        return sx, lax.div(sy, 2)

    def d_copy(dev):
        return remote(l_ref, ii.at[x, col], d_send.at[0], d_recv.at[x, h], dev)

    def z_copy(up, n, phase):
        p, u = lax.div(n, UNITS), lax.rem(n, UNITS)
        sx, sh = z_piece(up, p)
        start = lax.div(u, 4) * (rows // 2) + sum(sizes[:phase])
        cut = pl.ds(pl.multiple_of(start, 8), sizes[phase])
        at = ii.at[sx, 2 * sh + b, cut]
        k = 0 if up else 1
        return remote(at, at, z_send.at[k, n], z_recv.at[k, n], device(dz=1 if up else 7))

    def ip_copy(sx, sh):
        at = ii.at[sx, 2 * sh + b]
        return remote(at, at, ip_send.at[sx, sh], ip_recv.at[sx, sh], partner)

    def z_step(up, m):
        t = t_up if up else t_down
        n = m - LAG * t
        phase = m % LAG

        if m < n_units:
            @pl.when(at_home)
            def _():
                if m % UNITS == 0:
                    sx, sh = z_piece(up, m // UNITS)
                    if up and m == 0:
                        own_home.wait()
                    else:
                        remote(l_ref, ii.at[sx, 2 * sh + b], d_send.at[0], d_recv.at[sx, sh], here).wait_recv()
                    ip_copy(sx, sh).start()
                z_copy(up, jnp.int32(m), phase).start()

        if m >= LAG:
            @pl.when((t > 0) & (n >= 0) & (n < n_units))
            def _():
                z_copy(up, n, phase).wait_recv()

                @pl.when(t < 7)
                def _():
                    z_copy(up, n, phase).start()

                if phase == LAG - 1:
                    @pl.when(lax.rem(n, UNITS) == UNITS - 1)
                    def _():
                        ip_copy(*z_piece(up, lax.div(n, UNITS))).start()

    own_home = pltpu.make_async_copy(l_ref, ii.at[x, col], local.at[0])
    own_j = pltpu.make_async_copy(l_ref, j_at(x, y), local.at[1])
    own_r = pltpu.make_async_copy(r_ref, rp.at[x, col], local.at[2])
    for i, dev in ((0, device(dy=2)), (1, partner)):
        n_own(i, dev).start()
        r_own(i, dev).start()

    @pl.when(at_home)
    def _():
        own_home.start()

    source_is_me = (lax.div(z, 2) == x) & (lax.rem(z, 2) == h)

    @pl.when(~source_is_me)
    def _():
        d_copy(source).start()

    own_j.start()
    own_r.start()
    panels[col] = n_ref[...]

    @pl.when(~source_is_me)
    def _():
        d_copy(source).wait_send()

    for e in (1, 3, 2):
        j_first(e).start()
    for d in (1, 3, 2):
        j_second(0, d).start()

    early = 8
    for step in range(early):
        z_step(True, step)
        z_step(False, step)
    own_j.wait()
    own_r.wait()
    j_arrive(0, 0)

    n_own(0, here).wait_recv()
    r_own(0, here).wait_recv()
    n_copy(2, far_c, partner).start()
    r_copy(2, far_c, partner).start()
    n_own(1, here).wait_recv()
    r_own(1, here).wait_recv()
    n_copy(2, last_c, here).wait_recv()
    r_copy(2, last_c, here).wait_recv()
    for d in (1, 3, 2):
        rx_copy(d).start()

    live = live_ref[arc_ref[0]]
    sub = lax.broadcasted_iota(jnp.int32, (512, 128), 0)
    lane = lax.broadcasted_iota(jnp.int32, (512, 128), 1)
    for c in range(4):
        ident = jnp.where(sub == lane + 128 * c, 1.0, 0.0)
        keep = (sub < live) & (lane + 128 * c < live)
        work[c] = jnp.where(keep, panels[c], ident)

    def first_arrival(e):
        j_arrive(e, 0)
        for d in (1, 3, 2):
            j_second(e, d).start()

    def ring(m):
        z_step(True, m)
        z_step(False, m)

    steps = n_units + 7 * LAG
    events = [functools.partial(ring, m) for m in range(early, steps)]
    for k, e in enumerate((1, 3, 2)):
        events.insert(2 * k, functools.partial(first_arrival, e))
    state = {"ticks": 0, "done": 0}

    def tick():
        state["ticks"] += 1
        n = state["ticks"]
        if n % 2 == 0 and state["done"] < len(events):
            events[state["done"]]()
            state["done"] += 1

    invert(work, tick)

    for half in range(2):
        for k, (r, c) in enumerate(PACK[half]):
            rs = slice(128 * r, 128 * r + 128)
            keep = (sub[rs] < live) & (lane[rs] + 128 * c < live)
            pk[x, half, 128 * k : 128 * k + 128, :] = jnp.where(keep, work[c, rs, :], 0.0)

    def v_copy(d):
        return remote(pk.at[x, b], pk.at[x, b], v_send.at[d], v_recv.at[d], device(dx=d))

    def v_slot(d):
        return lax.rem(x - d + 4, 4)

    def v_arrive(d):
        at = pk.at[v_slot(d), b]
        remote(at, at, v_send.at[0], v_recv.at[d], here).wait_recv()

    def v_pass(d):
        at = pk.at[v_slot(d), b]
        return remote(at, at, vp_send.at[d], vp_recv.at[d], partner)

    def v_passed(d):
        at = pk.at[v_slot(d), 1 - b]
        remote(at, at, vp_send.at[0], vp_recv.at[d], here).wait_recv()

    for d in (1, 3, 2):
        v_copy(d).start()

    def split_j(s, c):
        at = slice(512 * s + 128 * c, 512 * s + 128 * c + 128)
        bh[:, at], bl[:, at] = split(jj[s, c, b])

    def j_passed(sx, sh):
        at = jj.at[sx, 2 * sh + (1 - b), b]
        remote(at, at, jp_send.at[0, 0], jp_recv.at[sx, sh], here).wait_recv()

    def build(s):
        for half in range(2):
            for k, (r, c) in enumerate(PACK[half]):
                block = pk[s, half, 128 * k : 128 * k + 128, :]
                rs, cs = slice(128 * r, 128 * r + 128), slice(128 * c, 128 * c + 128)
                nh[s, rs, cs], nl[s, rs, cs] = split(block)
                if r != c:
                    nh[s, cs, rs], nl[s, cs, rs] = split(block.T)

    def v_get(d):
        v_arrive(d)
        v_pass(d).start()
        rx_s = rp.at[v_slot(d)]
        remote(rx_s, rx_s, rx_send.at[0], rx_recv.at[d], here).wait_recv()

    def v_use(d):
        v_passed(d)
        build(v_slot(d))

    fill = [functools.partial(j_arrive, e, d) for e in (0, 1, 3, 2) for d in (1, 3, 2)]
    fill += [functools.partial(j_passed, sx, sh) for sx in range(4) for sh in range(2)]
    fill += [functools.partial(split_j, s, c) for s in range(4) for c in range(4)]
    fill.append(lambda: build(x))
    for d in (1, 3, 2):
        fill.append(functools.partial(v_get, d))
    for d in (1, 3, 2):
        fill.append(functools.partial(v_use, d))
    left = events[state["done"] :]
    for k, event in enumerate(left):
        event()
        for f in fill[-(-len(fill) * k // len(left)) : -(-len(fill) * (k + 1) // len(left))]:
            f()

    for sx in range(4):
        for sh in range(2):
            at = ii.at[sx, 2 * sh + (1 - b)]
            remote(at, at, ip_send.at[0, 0], ip_recv.at[sx, sh], here).wait_recv()
    for s in range(4):
        for c in range(4):
            at = slice(512 * s + 128 * c, 512 * s + 128 * c + 128)
            ah[0:rows, at], al[0:rows, at] = split(ii[s, c])
            ah[rows : rows + 16, at], al[rows : rows + 16, at] = split(
                jnp.broadcast_to(rp[s, c], (16, 128))
            )

    total = rows + 16
    parts = (slice(0, total // 2), slice(total // 2, total))

    def swap(k):
        return remote(tile.at[parts[k]], other.at[parts[k]], t_send.at[k], t_recv.at[k], swap_to)

    def out_copies(k, src):
        if k == 0:
            return [pltpu.make_async_copy(src.at[parts[0]], out_ref.at[parts[0]], local.at[3])]
        return [
            pltpu.make_async_copy(
                src.at[total // 2 : rows], out_ref.at[total // 2 : rows], local.at[4]
            ),
            pltpu.make_async_copy(src.at[rows : rows + 8], rhs_ref, local.at[5]),
        ]

    for k in range(2):
        cut = parts[k]
        for s in range(4):
            at = slice(512 * s, 512 * s + 512)
            w = dot3((ah[cut, at], al[cut, at]), (nh[s], nl[s]), ((1,), (0,)))
            wh[cut, at], wl[cut, at] = split(w)
        tile[cut] = dot3((wh[cut], wl[cut]), (bh[...], bl[...]), ((1,), (1,)))

        @pl.when(l != b)
        def _():
            swap(k).start()

        @pl.when(l == b)
        def _():
            for c in out_copies(k, tile):
                c.start()

    for k in range(2):
        @pl.when(l != b)
        def _():
            swap(k).wait()
            for c in out_copies(k, other):
                c.start()

    for k in range(2):
        for c in out_copies(k, other):
            c.wait()

    n_own(0, partner).wait_send()
    n_own(1, partner).wait_send()
    r_own(0, partner).wait_send()
    r_own(1, partner).wait_send()
    n_copy(2, far_c, partner).wait_send()
    r_copy(2, far_c, partner).wait_send()

    for e in (1, 2, 3):
        j_first(e).wait_send()
        rx_copy(e).wait_send()
    for e in range(4):
        for d in (1, 2, 3):
            j_second(e, d).wait_send()
    for sx in range(4):
        for sh in range(2):
            jp_copy(sx, sh).wait_send()
            ip_copy(sx, sh).wait_send()
    for n in range(n_units):
        for up in (True, False):
            @pl.when((t_up if up else t_down) < 7)
            def _():
                z_copy(up, jnp.int32(n), n % LAG).wait_send()
    for d in (1, 2, 3):
        v_copy(d).wait_send()
        v_pass(d).wait_send()


def shards(local_normal, link_block, local_rhs, arc_of_slot, live_params):
    order, width = local_normal.shape[1:]
    rows = link_block.shape[1]
    vmem = pl.BlockSpec(memory_space=pltpu.VMEM)
    smem = pl.BlockSpec(memory_space=pltpu.SMEM)
    dma = pltpu.SemaphoreType.DMA
    piece = (rows, width)
    wide = 4 * order
    tile, vector = pl.pallas_call(
        kernel,
        out_shape=(
            jax.ShapeDtypeStruct((rows, rows), F32),
            jax.ShapeDtypeStruct((8, rows), F32),
        ),
        in_specs=[smem, smem, vmem, vmem, vmem],
        out_specs=(pl.BlockSpec(memory_space=pl.ANY),) * 2,
        scratch_shapes=[
            pltpu.VMEM((4, order, width), F32),
            pltpu.VMEM((4, 4, 1, width), F32),
            pltpu.VMEM((4, order, width), F32),
            pltpu.VMEM((4, 4, 2) + piece, F32),
            pltpu.VMEM((4, 4) + piece, F32),
            pltpu.VMEM((4, 2, 5 * width, width), F32),
            pltpu.VMEM((rows + 16, wide), BF16),
            pltpu.VMEM((rows + 16, wide), BF16),
            pltpu.VMEM((rows, wide), BF16),
            pltpu.VMEM((rows, wide), BF16),
            pltpu.VMEM((4, order, order), BF16),
            pltpu.VMEM((4, order, order), BF16),
            pltpu.VMEM((rows + 16, wide), BF16),
            pltpu.VMEM((rows + 16, wide), BF16),
            pltpu.VMEM((rows + 16, rows), F32),
            pltpu.VMEM((rows + 16, rows), F32),
            dma((3,)), dma((3,)), dma((3,)), dma((3,)), dma((4,)), dma((4,)),
            dma((1,)), dma((4, 2)), dma((20,)), dma((16,)),
            dma((4, 2)), dma((4, 2)), dma((2, 4 * UNITS)), dma((2, 4 * UNITS)), dma((4, 2)), dma((4, 2)),
            dma((4,)), dma((4,)), dma((4,)), dma((4,)), dma((2,)), dma((2,)), dma((6,)),
        ],
        compiler_params=pltpu.CompilerParams(
            collective_id=0, has_side_effects=True, vmem_limit_bytes=56 * 2**20
        ),
        name="eliminate",
    )(arc_of_slot, live_params, local_normal[0], link_block[0], local_rhs)
    return tile, vector[0]


def solution(mesh):
    in_specs = (P("arc", None, "col"), P("arc", "row", "col"), P("arc", "col"), P("arc"), P())
    out_specs = (P(("arc", "col"), "row"), P("row"))
    return jax.shard_map(
        shards, mesh=mesh, in_specs=in_specs, out_specs=out_specs, check_vma=False
    )
```

time: 143 us -> 118 us (0.83)
  the two profiles are of different devices: /device:TPU:24 before, /device:TPU:33 now
where the time goes in v2:
time: 118 us; the launch traced here: 117 us
  Pallas kernels  113 us (96%)
  local copies, waits for them, and re-layouts  3.48 us (3%)
  between operations  1.29 us (1%)
    pallas_call x1, Pallas kernels, shards(): pl.pallas_call(kernel, out_shape=(jax.ShapeDtypeStruct((rows, rows), F32)...  113 us

profile of v2, /device:TPU:33, one launch (start us, length us, event | category | flops | bytes accessed | tf_op | source)
XLA Modules:
  0.0 117.5 jit_solution(7111473865587521345)
XLA Ops:
  1.3 112.7 %eliminate.1 = (f32[464,464]{1,0:T(8,128)}, f32[8,464]{1,0:T(8,128)}) custom-call(s32[1]{0:T(128)S(6)} %copy.8.arc_ref, s32[4]{0:T(128)} %live_ref.1, f32[512,128]{1,0:T(8,128)} %bitcast.3, f32[464,128]{1,0:T(8,128)} %bitcast.4, f32[1,128]{1,0:T(1,128)} %r_ref.1), custom_call_target="tpu_custom_call" | custom-call | tf_op jit(solution)/shard_map/eliminate/pallas_call | solution.py:491
  114.0 1.3 %slice.3 = f32[1,464]{1,0:T(1,128)} slice(f32[8,464]{1,0:T(8,128)} %get-tuple-element.5), slice={[0:1], [0:464]} | slice | bytes 3712 | tf_op jit(solution)/shard_map/slice | solution.py:526
  115.3 2.2 %copy.9 = f32[464,464]{1,0:T(8,128)} copy(f32[464,464]{1,0:T(8,128)} %get-tuple-element.8) | data formatting | bytes 1722368

commit v3 on v2

--- a/solution.py
+++ b/solution.py
@@ -10,8 +10,6 @@
 HI = lax.Precision.HIGHEST
 F32 = jnp.float32
 BF16 = jnp.bfloat16
-UNITS = 8
-LAG = 4
 PACK = (((0, 0), (1, 0), (2, 0), (3, 0), (3, 3)), ((1, 1), (2, 1), (3, 1), (2, 2), (3, 2)))
 
 
@@ -94,9 +92,9 @@
 
 def kernel(
     arc_ref, live_ref, n_ref, l_ref, r_ref, out_ref, rhs_ref,
-    panels, rp, work, jj, ii, pk, ah, al, bh, bl, nh, nl, wh, wl, tile, other,
-    n_send, n_recv, r_send, r_recv, rx_send, rx_recv, d_send, d_recv, j_send, j_recv,
-    jp_send, jp_recv, z_send, z_recv, ip_send, ip_recv,
+    panels, rp, work, jj, zb, ii, pk, ah, al, bh, bl, nh, nl, wh, wl, tile, other,
+    n_send, n_recv, r_send, r_recv, rx_send, rx_recv, j_send, j_recv,
+    jp_send, jp_recv, z_send, z_recv, i_send, i_recv, ip_send, ip_recv,
     v_send, v_recv, vp_send, vp_recv, t_send, t_recv, local,
 ):
     x = lax.axis_index("arc")
@@ -106,7 +104,6 @@
     h, b = lax.div(col, 2), lax.rem(col, 2)
     y = 2 * h + l
     home = 2 * x + h
-    at_home = z == home
     rows = l_ref.shape[0]
 
     def device(dx=0, dy=0, dz=0, db=0):
@@ -127,7 +124,6 @@
 
     here = {"arc": x, "row": row, "col": col}
     swap_to = {"arc": x, "row": 2 * z + (1 - l), "col": 2 * h + (1 - b)}
-    source = {"arc": lax.div(z, 2), "row": row, "col": 2 * lax.rem(z, 2) + b}
     partner = device(db=1)
 
     barrier = pltpu.get_barrier_semaphore()
@@ -190,101 +186,96 @@
         def _():
             jp_copy(sx, lax.div(sy, 2)).start()
 
-    t_up = lax.rem(z - home + 8, 8)
-    t_down = lax.rem(home - z + 8, 8)
-    n_units = 4 * UNITS
-    quarter = rows // 2 // 4 // 8 * 8
-    sizes = (rows // 2 - 3 * quarter, quarter, quarter, quarter)
-
-    def z_piece(up, p):
-        dx = lax.rem(p, 2) if up else 3 - lax.rem(p, 2)
-        sx, sy = slot_of(dx, 2 * lax.div(p, 2))
-        return sx, lax.div(sy, 2)
-
-    def d_copy(dev):
-        return remote(l_ref, ii.at[x, col], d_send.at[0], d_recv.at[x, h], dev)
-
-    def z_copy(up, n, phase):
-        p, u = lax.div(n, UNITS), lax.rem(n, UNITS)
-        sx, sh = z_piece(up, p)
-        start = lax.div(u, 4) * (rows // 2) + sum(sizes[:phase])
-        cut = pl.ds(pl.multiple_of(start, 8), sizes[phase])
-        at = ii.at[sx, 2 * sh + b, cut]
-        k = 0 if up else 1
-        return remote(at, at, z_send.at[k, n], z_recv.at[k, n], device(dz=1 if up else 7))
+    half_rows = rows // 2
+
+    def z_slot(up, k):
+        return lax.rem(z + (8 - k if up else k), 8)
+
+    def z_copy(up, k, part):
+        q = z_slot(up, k - 1)
+        cut = pl.ds(part * half_rows, half_rows)
+        src = l_ref.at[cut] if k == 1 else zb.at[q, cut]
+        i = 0 if up else 1
+        return remote(
+            src, zb.at[q, cut], z_send.at[i, k - 1, part], z_recv.at[i, k - 1, part],
+            device(dz=1 if up else 7),
+        )
+
+    def z_arrive(up, k, part):
+        q = z_slot(up, k)
+        cut = pl.ds(part * half_rows, half_rows)
+        i = 0 if up else 1
+        remote(
+            zb.at[q, cut], zb.at[q, cut], z_send.at[0, 0, 0], z_recv.at[i, k - 1, part], here
+        ).wait_recv()
+        if k < 3 or k == 3 and part == i:
+            z_copy(up, k + 1, part).start()
+
+    def i_copy(q, src):
+        user = {"arc": lax.div(q, 2), "row": row, "col": 2 * lax.rem(q, 2) + b}
+        return remote(src, ii.at[x, col], i_send.at[q], i_recv.at[x, h], user)
+
+    def i_local(src):
+        return pltpu.make_async_copy(src, ii.at[x, col], local.at[0])
+
+    def i_start(q, src):
+        @pl.when(q == home)
+        def _():
+            i_local(src).start()
+
+        @pl.when(q != home)
+        def _():
+            i_copy(q, src).start()
 
     def ip_copy(sx, sh):
         at = ii.at[sx, 2 * sh + b]
         return remote(at, at, ip_send.at[sx, sh], ip_recv.at[sx, sh], partner)
 
-    def z_step(up, m):
-        t = t_up if up else t_down
-        n = m - LAG * t
-        phase = m % LAG
-
-        if m < n_units:
-            @pl.when(at_home)
-            def _():
-                if m % UNITS == 0:
-                    sx, sh = z_piece(up, m // UNITS)
-                    if up and m == 0:
-                        own_home.wait()
-                    else:
-                        remote(l_ref, ii.at[sx, 2 * sh + b], d_send.at[0], d_recv.at[sx, sh], here).wait_recv()
-                    ip_copy(sx, sh).start()
-                z_copy(up, jnp.int32(m), phase).start()
-
-        if m >= LAG:
-            @pl.when((t > 0) & (n >= 0) & (n < n_units))
-            def _():
-                z_copy(up, n, phase).wait_recv()
-
-                @pl.when(t < 7)
-                def _():
-                    z_copy(up, n, phase).start()
-
-                if phase == LAG - 1:
-                    @pl.when(lax.rem(n, UNITS) == UNITS - 1)
-                    def _():
-                        ip_copy(*z_piece(up, lax.div(n, UNITS))).start()
-
-    own_home = pltpu.make_async_copy(l_ref, ii.at[x, col], local.at[0])
+    def i_arrive(dx, dh):
+        sx, sy = slot_of(dx, 2 * dh)
+        sh = lax.div(sy, 2)
+        if dx or dh:
+            at = ii.at[sx, 2 * sh + b]
+            remote(at, at, i_send.at[0], i_recv.at[sx, sh], here).wait_recv()
+        else:
+            i_local(l_ref).wait()
+        ip_copy(sx, sh).start()
+
+    def z_event(k, part):
+        if k < 4:
+            for up in (True, False):
+                z_arrive(up, k, part)
+                if part:
+                    i_start(z_slot(up, k), zb.at[z_slot(up, k)])
+        else:
+            z_arrive(True, 4, 0)
+            z_arrive(False, 4, 1)
+            i_start(z_slot(True, 4), zb.at[z_slot(True, 4)])
+
     own_j = pltpu.make_async_copy(l_ref, j_at(x, y), local.at[1])
     own_r = pltpu.make_async_copy(r_ref, rp.at[x, col], local.at[2])
     for i, dev in ((0, device(dy=2)), (1, partner)):
         n_own(i, dev).start()
         r_own(i, dev).start()
 
-    @pl.when(at_home)
-    def _():
-        own_home.start()
-
-    source_is_me = (lax.div(z, 2) == x) & (lax.rem(z, 2) == h)
-
-    @pl.when(~source_is_me)
-    def _():
-        d_copy(source).start()
-
+    for part in range(2):
+        for up in (True, False):
+            z_copy(up, 1, part).start()
     own_j.start()
     own_r.start()
     panels[col] = n_ref[...]
-
-    @pl.when(~source_is_me)
-    def _():
-        d_copy(source).wait_send()
 
     for e in (1, 3, 2):
         j_first(e).start()
     for d in (1, 3, 2):
         j_second(0, d).start()
 
-    early = 8
-    for step in range(early):
-        z_step(True, step)
-        z_step(False, step)
+    i_start(z, l_ref)
     own_j.wait()
     own_r.wait()
     j_arrive(0, 0)
+    z_event(1, 0)
+    z_event(1, 1)
 
     n_own(0, here).wait_recv()
     r_own(0, here).wait_recv()
@@ -310,22 +301,15 @@
         for d in (1, 3, 2):
             j_second(e, d).start()
 
-    def ring(m):
-        z_step(True, m)
-        z_step(False, m)
-
-    steps = n_units + 7 * LAG
-    events = [functools.partial(ring, m) for m in range(early, steps)]
-    for k, e in enumerate((1, 3, 2)):
-        events.insert(2 * k, functools.partial(first_arrival, e))
-    state = {"ticks": 0, "done": 0}
+    events = {2 + 2 * k: functools.partial(first_arrival, e) for k, e in enumerate((1, 3, 2))}
+    for n, k, part in ((12, 2, 0), (20, 2, 1), (29, 3, 0), (38, 3, 1), (52, 4, 0)):
+        events[n] = functools.partial(z_event, k, part)
+    state = {"ticks": 0}
 
     def tick():
         state["ticks"] += 1
-        n = state["ticks"]
-        if n % 2 == 0 and state["done"] < len(events):
-            events[state["done"]]()
-            state["done"] += 1
+        if state["ticks"] in events:
+            events[state["ticks"]]()
 
     invert(work, tick)
 
@@ -341,9 +325,21 @@
     def v_slot(d):
         return lax.rem(x - d + 4, 4)
 
+    def v_relay(d):
+        length = pk.shape[2] // 2
+        at = pk.at[v_slot(d), b, pl.ds(0 if d == 1 else length, length)]
+        k = 0 if d == 1 else 2
+        return remote(at, at, v_send.at[k], v_recv.at[k], device(dx=d))
+
     def v_arrive(d):
-        at = pk.at[v_slot(d), b]
-        remote(at, at, v_send.at[0], v_recv.at[d], here).wait_recv()
+        if d == 2:
+            for k in (0, 2):
+                at = pk.at[v_slot(2), b, pl.ds(0, pk.shape[2] // 2)]
+                remote(at, at, v_send.at[0], v_recv.at[k], here).wait_recv()
+        else:
+            at = pk.at[v_slot(d), b]
+            remote(at, at, v_send.at[0], v_recv.at[d], here).wait_recv()
+            v_relay(d).start()
 
     def v_pass(d):
         at = pk.at[v_slot(d), b]
@@ -353,7 +349,7 @@
         at = pk.at[v_slot(d), 1 - b]
         remote(at, at, vp_send.at[0], vp_recv.at[d], here).wait_recv()
 
-    for d in (1, 3, 2):
+    for d in (1, 3):
         v_copy(d).start()
 
     def split_j(s, c):
@@ -384,18 +380,15 @@
         build(v_slot(d))
 
     fill = [functools.partial(j_arrive, e, d) for e in (0, 1, 3, 2) for d in (1, 3, 2)]
+    fill += [functools.partial(v_get, d) for d in (1, 3)]
     fill += [functools.partial(j_passed, sx, sh) for sx in range(4) for sh in range(2)]
     fill += [functools.partial(split_j, s, c) for s in range(4) for c in range(4)]
-    fill.append(lambda: build(x))
-    for d in (1, 3, 2):
-        fill.append(functools.partial(v_get, d))
-    for d in (1, 3, 2):
-        fill.append(functools.partial(v_use, d))
-    left = events[state["done"] :]
-    for k, event in enumerate(left):
-        event()
-        for f in fill[-(-len(fill) * k // len(left)) : -(-len(fill) * (k + 1) // len(left))]:
-            f()
+    fill.append(functools.partial(build, x))
+    fill += [functools.partial(i_arrive, dx, dh) for dh in (0, 1) for dx in (0, 1, 3, 2)]
+    fill.append(functools.partial(v_get, 2))
+    fill += [functools.partial(v_use, d) for d in (1, 3, 2)]
+    for f in fill:
+        f()
 
     for sx in range(4):
         for sh in range(2):
@@ -470,13 +463,20 @@
         for sh in range(2):
             jp_copy(sx, sh).wait_send()
             ip_copy(sx, sh).wait_send()
-    for n in range(n_units):
-        for up in (True, False):
-            @pl.when((t_up if up else t_down) < 7)
-            def _():
-                z_copy(up, jnp.int32(n), n % LAG).wait_send()
+    for up in (True, False):
+        for k in (1, 2, 3, 4):
+            for part in range(2):
+                if k < 4 or part == (0 if up else 1):
+                    z_copy(up, k, part).wait_send()
+    for q in range(8):
+        @pl.when(home != q)
+        def _():
+            i_copy(q, l_ref).wait_send()
+
+    for d in (1, 3):
+        v_copy(d).wait_send()
+        v_relay(d).wait_send()
     for d in (1, 2, 3):
-        v_copy(d).wait_send()
         v_pass(d).wait_send()
 
 
@@ -501,6 +501,7 @@
             pltpu.VMEM((4, 4, 1, width), F32),
             pltpu.VMEM((4, order, width), F32),
             pltpu.VMEM((4, 4, 2) + piece, F32),
+            pltpu.VMEM((8,) + piece, F32),
             pltpu.VMEM((4, 4) + piece, F32),
             pltpu.VMEM((4, 2, 5 * width, width), F32),
             pltpu.VMEM((rows + 16, wide), BF16),
@@ -514,8 +515,8 @@
             pltpu.VMEM((rows + 16, rows), F32),
             pltpu.VMEM((rows + 16, rows), F32),
             dma((3,)), dma((3,)), dma((3,)), dma((3,)), dma((4,)), dma((4,)),
-            dma((1,)), dma((4, 2)), dma((20,)), dma((16,)),
-            dma((4, 2)), dma((4, 2)), dma((2, 4 * UNITS)), dma((2, 4 * UNITS)), dma((4, 2)), dma((4, 2)),
+            dma((20,)), dma((16,)),
+            dma((4, 2)), dma((4, 2)), dma((2, 4, 2)), dma((2, 4, 2)), dma((8,)), dma((4, 2)), dma((4, 2)), dma((4, 2)),
             dma((4,)), dma((4,)), dma((4,)), dma((4,)), dma((2,)), dma((2,)), dma((6,)),
         ],
         compiler_params=pltpu.CompilerParams(

time: 118 us -> 108 us (0.915)
  the two profiles are of different devices: /device:TPU:33 before, /device:TPU:1 now
where the time goes in v3:
time: 108 us; the launch traced here: 107 us
  Pallas kernels  103 us (95%)
  local copies, waits for them, and re-layouts  3.48 us (3%)
  between operations  1.29 us (1%)
    pallas_call x1, Pallas kernels, shards(): pl.pallas_call(kernel, out_shape=(jax.ShapeDtypeStruct((rows, rows), F32)...  103 us
    unnamed x1, local copies, waits for them, and re-layouts  2.19 us

profile of v3, /device:TPU:1, one launch (start us, length us, event | category | flops | bytes accessed | tf_op | source)
XLA Modules:
  0.0 107.3 jit_solution(14930430048150970347)
XLA Ops:
  1.3 102.6 %eliminate.1 = (f32[464,464]{1,0:T(8,128)}, f32[8,464]{1,0:T(8,128)}) custom-call(s32[1]{0:T(128)S(6)} %copy.8.arc_ref, s32[4]{0:T(128)} %live_ref.1, f32[512,128]{1,0:T(8,128)} %bitcast.3, f32[464,128]{1,0:T(8,128)} %bitcast.4, f32[1,128]{1,0:T(1,128)} %r_ref.1), custom_call_target="tpu_custom_call" | custom-call | tf_op jit(solution)/shard_map/eliminate/pallas_call | solution.py:491
  103.9 1.3 %slice.3 = f32[1,464]{1,0:T(1,128)} slice(f32[8,464]{1,0:T(8,128)} %get-tuple-element.5), slice={[0:1], [0:464]} | slice | bytes 3712 | tf_op jit(solution)/shard_map/slice | solution.py:527
  105.2 2.2 %copy.9 = f32[464,464]{1,0:T(8,128)} copy(f32[464,464]{1,0:T(8,128)} %get-tuple-element.8) | data formatting | bytes 1722368

commit v4 on v3

--- a/solution.py
+++ b/solution.py
@@ -415,7 +415,7 @@
             pltpu.make_async_copy(
                 src.at[total // 2 : rows], out_ref.at[total // 2 : rows], local.at[4]
             ),
-            pltpu.make_async_copy(src.at[rows : rows + 8], rhs_ref, local.at[5]),
+            pltpu.make_async_copy(src.at[rows : rows + 1], rhs_ref, local.at[5]),
         ]
 
     for k in range(2):
@@ -492,7 +492,7 @@
         kernel,
         out_shape=(
             jax.ShapeDtypeStruct((rows, rows), F32),
-            jax.ShapeDtypeStruct((8, rows), F32),
+            jax.ShapeDtypeStruct((1, rows), F32),
         ),
         in_specs=[smem, smem, vmem, vmem, vmem],
         out_specs=(pl.BlockSpec(memory_space=pl.ANY),) * 2,
@@ -524,7 +524,7 @@
         ),
         name="eliminate",
     )(arc_of_slot, live_params, local_normal[0], link_block[0], local_rhs)
-    return tile, vector[0]
+    return tile, vector.reshape(rows)
 
 
 def solution(mesh):

time: 108 us -> 107 us (level)
    slice x1 -> x0, local copies, waits for them, and re-layouts: 1.3 us -> none  [shards(): return (tile, vector[0])]
    unnamed x1 -> x4, local copies, waits for them, and re-layouts: 2.19 us -> 2.77 us
where the time goes in v4:
time: 107 us
  Pallas kernels  103 us (96%)
  local copies, waits for them, and re-layouts  2.77 us (3%)
  between operations  1.29 us (1%)
    pallas_call x1, Pallas kernels, shards(): pl.pallas_call(kernel, out_shape=(jax.ShapeDtypeStruct((rows, rows), F32)...  103 us
    unnamed x4, local copies, waits for them, and re-layouts  2.77 us

profile of v4, /device:TPU:1, one launch (start us, length us, event | category | flops | bytes accessed | tf_op | source)
XLA Modules:
  0.0 106.6 jit_solution(17574884523443342487)
XLA Ops:
  1.3 102.6 %eliminate.1 = (f32[464,464]{1,0:T(8,128)}, f32[1,464]{1,0:T(1,128)}) custom-call(s32[1]{0:T(128)S(6)} %copy.9.arc_ref, s32[4]{0:T(128)} %live_ref.1, f32[512,128]{1,0:T(8,128)} %bitcast.3, f32[464,128]{1,0:T(8,128)} %bitcast.4, f32[1,128]{1,0:T(1,128)} %r_ref.1), custom_call_target="tpu_custom_call" | custom-call | tf_op jit(solution)/shard_map/eliminate/pallas_call | solution.py:491
  103.8 0.0 copy-start
  103.9 2.2 %copy.10 = f32[464,464]{1,0:T(8,128)} copy(f32[464,464]{1,0:T(8,128)} %get-tuple-element.8) | data formatting | bytes 1722368
  106.0 0.0 copy-done
  106.0 0.6 copy.11
Async XLA Ops:
  103.8 2.2 %copy-start = (f32[1,464]{1,0:T(1,128)S(1)}, f32[1,464]{1,0:T(1,128)}, u32[]{:S(2)}) copy-start(f32[1,464]{1,0:T(1,128)} %get-tuple-element.5) | copy-start | bytes 5572
